TPU v7x, 32 devices: a whole 2x2x4 slice. The times are simulated.
32 devices in a mesh: scan: 2 (over y), ang: 4 (over z), row: 4 (over x, core).
Axes of the slice: x: 2, y: 2, z: 4, core: 2. Of those that a mesh axis runs over, the one named last changes fastest.
Arguments:
- raw_frames: bfloat16 [96, 128, 2560], P(('scan', 'ang'), 'row'), parts along dimension 0, may hold values from 0.099609375 to 1.5
- dark_field: bfloat16 [128, 2560], P('row'), may hold values from 0 to 0.079589844
- flat_field: bfloat16 [128, 2560], P('row'), may hold values from 0.796875 to 1.1953125
- kernel_taps: float32 [31], replicated, may hold values from 0.1 to 0.4
- partner: int32 [48], P('scan'), parts along dimension 0, may hold values from 24 to 47, as said below
- shifts: int32 [256], replicated, may hold values from -256 to 255, as said below
Outputs:
- sinograms: bfloat16 [96, 128, 2560], P('scan', ('ang', 'row')), parts along dimension 0
- correlation: float32 [256, 256], P(('scan', 'ang', 'row')), parts along dimension 0
There are 2 independent parts, one for each index of `scan`. A program takes and returns all parts, laid end to end along the dimension named above; an argument that names none is the same for every part. Nothing has to cross between parts.
Inputs may be any that keep to these rules, and one draw needn't show every extreme that they name: partner[i] - i - 24 is -1, 0 or 1 for every i; partner[0] = 24 and partner[23] = 47. shifts[0] = -256 and shifts[255] = 255; values may repeat.
All inputs are finite; a program needn't handle non-finite values.
Results may differ from a plain program's by a relative error of at most 0.012.
The roundings to bfloat16 on the way count: a program that leaves them out, or rounds other values in their place, can miss the bound.
Values may be sent and summed in bfloat16 or wider, within the bound.
A program may use at most 128 MiB of HBM per device.

v0:
```python
import functools
import math

import jax
import jax.numpy as jnp
from jax import lax
from jax.experimental import pallas as pl
from jax.experimental.pallas import tpu as pltpu
from jax.sharding import PartitionSpec as P

SPAN = 256
LANES = 128
TILE = 256
CORES = 2
MESH = pl.DeviceIdType.MESH


def split(value):
    high = value.astype(jnp.bfloat16)
    low = (value - high.astype(jnp.float32)).astype(jnp.bfloat16)
    return high, low


def band(taps_ref, lag, rows_same=None):
    tap_count = taps_ref.shape[0]
    total = jnp.zeros(lag.shape, jnp.float32)
    for tap_index in range(tap_count):
        total = jnp.where(lag == tap_index, taps_ref[tap_index], total)
    if rows_same is not None:
        total = jnp.where(rows_same, total, 0.0)
    return total


def dot(left, right):
    return jnp.dot(left, right, preferred_element_type=jnp.float32)


def ramp_block(offset):
    shape = (TILE, TILE)
    distance = (
        lax.broadcasted_iota(jnp.int32, shape, 0)
        - lax.broadcasted_iota(jnp.int32, shape, 1)
        + offset
    )
    spacing = distance.astype(jnp.float32)
    odd_distance = (distance & 1) != 0
    falloff = -4.0 / (math.pi * math.pi * jnp.maximum(spacing * spacing, 1.0))
    kernel = jnp.where(distance == 0, 1.0, jnp.where(odd_distance, falloff, 0.0))
    return kernel.astype(jnp.bfloat16)


def unpack(g, planes, group, share, ang_count, lines_ref, x_ref, rows_ref):
    parts = x_ref.shape[0]
    size = group * share
    for a in range(ang_count):
        first = a * planes + g * group
        for p in range(group):
            line = lines_ref[first + p].astype(jnp.float32)
            for q in range(parts):
                x_ref[q, pl.ds((first + p) * share, share)] = line[:, q * LANES : (q + 1) * LANES]
        for q in range(parts):
            rows_ref[pl.ds(a * size, size), pl.ds(q * LANES, LANES)] = x_ref[
                q, pl.ds(first * share, size)
            ].astype(jnp.bfloat16)


def match(share, partner_ref, shifts_ref, corr_ref, x_ref, b_ref, prof_ref):
    parts, count, _ = x_ref.shape
    half = count // share // 2
    cols = parts * LANES
    pad = SPAN // LANES
    for v in range(pad):
        b_ref[v] = jnp.zeros(b_ref.shape[1:], jnp.float32)
        b_ref[pad + parts + v] = jnp.zeros(b_ref.shape[1:], jnp.float32)

    def pick(i, carry):
        offset = partner_ref[i] - i - half
        middle = half + i

        def line(index):
            return x_ref[:, pl.ds(pl.multiple_of(index * share, share), share)]

        following = line(jnp.minimum(middle + 1, 2 * half - 1))
        chosen = jnp.where(offset > 0, following, line(middle))
        place = pl.multiple_of(i * share, share)
        b_ref[pl.ds(pad, parts), pl.ds(place, share)] = jnp.where(
            offset < 0, line(middle - 1), chosen
        )
        return carry

    lax.fori_loop(0, half, pick, 0)
    width = 2 * SPAN + LANES
    for r in range(share):
        rows = pl.ds(r, half, stride=share)
        left = jnp.concatenate(
            [x_ref[q, rows] for q in range(parts)], axis=0
        ).astype(jnp.bfloat16)
        pieces = [b_ref[v, rows] for v in range(parts + 2 * pad)]
        first = parts - 1
        right = jnp.concatenate(
            [
                jnp.concatenate([pieces[first - q + v] for q in range(parts)], axis=0)
                for v in range(width // LANES)
            ],
            axis=1,
        ).astype(jnp.bfloat16)
        product = lax.dot_general(
            left, right, (((0,), (0,)), ((), ())), preferred_element_type=jnp.float32
        )
        skewed = pltpu.roll(product, 0, 1, stride=1, stride_axis=0)
        prof_ref[pl.ds(r, 1)] = jnp.sum(skewed, axis=0, keepdims=True)[:, LANES:]

    lane = lax.broadcasted_iota(jnp.int32, (2 * SPAN, shifts_ref.shape[1]), 0)
    selector = (SPAN - 1 - lane == shifts_ref[...]).astype(jnp.float32)
    corr_ref[...] = jnp.dot(
        prof_ref[...],
        selector,
        precision=lax.Precision.HIGHEST,
        preferred_element_type=jnp.float32,
    ) * ((half * cols) ** -0.5)


def filter_kernel(
    sizes,
    taps_ref,
    raw_ref,
    dark_ref,
    flat_ref,
    partner_ref,
    shifts_ref,
    out_ref,
    corr_ref,
    lines_ref,
    halo_ref,
    level_ref,
    dark_ext,
    gain_ext,
    row_band,
    col_band,
    x_high,
    x_low,
    z_high,
    z_low,
    low_ref,
    send_ref,
    relay_ref,
    strip_ref,
    x_ref,
    rows_ref,
    b_ref,
    prof_ref,
    level_send,
    level_recv,
    halo_send,
    halo_recv,
    out_send,
    out_recv,
    relay_send,
    relay_recv,
):
    ang_count, row_devices, halo, group, joined = sizes
    planes, rows, cols = raw_ref.shape
    margin = taps_ref.shape[0] // 2
    groups = planes // group
    dests, _, share, _ = send_ref.shape
    ext = rows + 2 * halo
    scan, ang, row = lax.axis_index("scan"), lax.axis_index("ang"), lax.axis_index("row")
    has = (row > 0, row < row_devices - 1)
    peer = (jnp.maximum(row - 1, 0), jnp.minimum(row + 1, row_devices - 1))

    barrier = pltpu.get_barrier_semaphore()
    for a in range(ang_count):
        for b in range(row_devices):

            @pl.when(jnp.logical_or(ang != a, row != b))
            def _():
                pl.semaphore_signal(barrier, inc=1, device_id=(scan, a, b), device_id_type=MESH)

    pl.semaphore_wait(barrier, ang_count * row_devices - 1)

    def level_copy(side, which):
        source = (dark_ref, flat_ref)[which]
        start = 0 if side == 0 else rows - halo
        return pltpu.make_async_remote_copy(
            src_ref=source.at[pl.ds(start, halo)],
            dst_ref=level_ref.at[1 - side, which],
            send_sem=level_send.at[side, which],
            recv_sem=level_recv.at[1 - side, which],
            device_id=(scan, ang, peer[side]),
            device_id_type=MESH,
        )

    def halo_copy(side, g):
        start = 0 if side == 0 else rows - halo
        return pltpu.make_async_remote_copy(
            src_ref=raw_ref.at[pl.ds(g * group, group), pl.ds(start, halo)],
            dst_ref=halo_ref.at[1 - side, pl.ds(g * group, group)],
            send_sem=halo_send.at[side, g],
            recv_sem=halo_recv.at[1 - side, g],
            device_id=(scan, ang, peer[side]),
            device_id_type=MESH,
        )

    def start_halo(g):
        for side in range(2):

            @pl.when(has[side])
            def _():
                halo_copy(side, g).start()

    for side in range(2):

        @pl.when(has[side])
        def _():
            for which in range(2):
                level_copy(side, which).start()

    for g in range(min(2, groups)):
        start_halo(g)

    out_rows = group * rows
    in_rows = group * ext
    r_out = lax.broadcasted_iota(jnp.int32, (out_rows, in_rows), 0)
    r_in = lax.broadcasted_iota(jnp.int32, (out_rows, in_rows), 1)
    lag = (r_in % ext) - (r_out % rows) - (halo - margin)
    high, low = split(band(taps_ref, lag, r_in // ext == r_out // rows))
    row_band[:out_rows] = high
    row_band[out_rows:] = low
    c_in = lax.broadcasted_iota(jnp.int32, (TILE + 2 * LANES, TILE), 0)
    c_out = lax.broadcasted_iota(jnp.int32, (TILE + 2 * LANES, TILE), 1)
    high, low = split(band(taps_ref, c_in - c_out - (LANES - margin)))
    col_band[:, :TILE] = high
    col_band[:, TILE:] = low
    for z_ref in (z_high, z_low):
        z_ref[:, :LANES] = jnp.zeros((out_rows, LANES), jnp.bfloat16)
        z_ref[:, LANES + cols :] = jnp.zeros((out_rows, LANES), jnp.bfloat16)

    def levels(dark, flat):
        dark = dark.astype(jnp.float32)
        return dark, jnp.log(flat.astype(jnp.float32) - dark)

    dark_ext[pl.ds(halo, rows)], gain_ext[pl.ds(halo, rows)] = levels(dark_ref[...], flat_ref[...])
    for side in range(2):

        @pl.when(has[side])
        def _():
            for which in range(2):
                level_copy(1 - side, which).wait_recv()

        at = 0 if side == 0 else halo + rows
        dark_ext[pl.ds(at, halo)], gain_ext[pl.ds(at, halo)] = levels(
            level_ref[side, 0], level_ref[side, 1]
        )

    upper = dests // row_devices

    def target(d):
        return upper * row + d // row_devices, d % row_devices

    def is_self(d):
        a, b = target(d)
        return jnp.logical_and(a == ang, b == row)

    def is_relayed(d):
        a, b = target(d)
        return jnp.logical_and(a != ang, b // CORES != row // CORES)

    def part(g):
        return pl.ds(g * group, group)

    def place(a, g):
        return lines_ref.at[pl.ds(a * planes + g * group, group)]

    def out_copy(d, g):
        a, b = target(d)
        return pltpu.make_async_remote_copy(
            src_ref=send_ref.at[d, part(g)],
            dst_ref=place(ang, g),
            send_sem=out_send.at[d, g],
            recv_sem=out_recv.at[ang, g],
            device_id=(scan, a, b),
            device_id_type=MESH,
        )

    def first_hop(d, g):
        return pltpu.make_async_remote_copy(
            src_ref=send_ref.at[d, part(g)],
            dst_ref=relay_ref.at[row, d // row_devices, part(g)],
            send_sem=out_send.at[d, g],
            recv_sem=relay_recv.at[row, d // row_devices, g],
            device_id=(scan, ang, d % row_devices),
            device_id_type=MESH,
        )

    def second_hop(b, u, g):
        return pltpu.make_async_remote_copy(
            src_ref=relay_ref.at[b, u, part(g)],
            dst_ref=place(ang, g),
            send_sem=relay_send.at[b, u, g],
            recv_sem=out_recv.at[ang, g],
            device_id=(scan, upper * b + u, row),
            device_id_type=MESH,
        )

    def own_copy(d, g):
        return pltpu.make_async_copy(send_ref.at[d, part(g)], place(ang, g), out_recv.at[ang, g])

    def relays(b, u):
        return jnp.logical_and(b // CORES != row // CORES, upper * b + u != ang)

    def each_relay(action):
        for b in range(row_devices):
            for u in range(upper):

                @pl.when(relays(b, u))
                def _():
                    action(b, u)

    def relay(g):
        def action(b, u):
            arrived = relay_ref.at[b, u, part(g)]
            pltpu.make_async_copy(arrived, arrived, relay_recv.at[b, u, g]).wait()
            second_hop(b, u, g).start()

        each_relay(action)

    def send(g):
        for d in range(dests):

            @pl.when(is_relayed(d))
            def _():
                first_hop(d, g).start()

        for d in range(dests):

            @pl.when(is_self(d))
            def _():
                own_copy(d, g).start()

            @pl.when(jnp.logical_not(jnp.logical_or(is_relayed(d), is_self(d))))
            def _():
                out_copy(d, g).start()

    for g in range(groups):
        for side in range(2):

            @pl.when(has[side])
            def _():
                halo_copy(1 - side, g).wait_recv()

        def absorb(p, carry):
            plane = g * group + p
            base = pl.multiple_of(p * ext, ext)

            def put(at, counts, valid):
                size = counts.shape[0]
                value = gain_ext[pl.ds(at, size)] - jnp.log(
                    counts.astype(jnp.float32) - dark_ext[pl.ds(at, size)]
                )
                if valid is not None:
                    value = jnp.where(valid, value, 0.0)
                high, low = split(value)
                x_high[pl.ds(base + at, size)] = high
                x_low[pl.ds(base + at, size)] = low

            put(0, halo_ref[0, plane], has[0])
            put(halo, raw_ref[plane], None)
            put(halo + rows, halo_ref[1, plane], has[1])
            return carry

        lax.fori_loop(0, group, absorb, 0)

        step = cols // 2 if cols // 2 % TILE == 0 else TILE

        def row_pass(n, carry):
            at = pl.multiple_of(n * step, TILE)
            both = dot(row_band[...], x_high[:, pl.ds(at, step)])
            rest = dot(row_band[:out_rows], x_low[:, pl.ds(at, step)])
            high, low = split(both[:out_rows] + (both[out_rows:] + rest))
            to = pl.multiple_of(n * step + LANES, LANES)
            z_high[:, pl.ds(to, step)] = high
            z_low[:, pl.ds(to, step)] = low
            return carry

        lax.fori_loop(0, cols // step, row_pass, 0)

        def windows(z_ref):
            return jnp.concatenate(
                [z_ref[:, n * TILE : (n + 1) * TILE + 2 * LANES] for n in range(cols // TILE)],
                axis=0,
            )

        both = dot(windows(z_high), col_band[...])
        rest = dot(windows(z_low), col_band[:, :TILE])
        value = both[:, :TILE] + (both[:, TILE:] + rest)
        total = jnp.zeros((out_rows, 1), jnp.float32)
        for n in range(cols // TILE):
            tile = value[n * out_rows : (n + 1) * out_rows]
            low_ref[:, n * TILE : (n + 1) * TILE] = tile
            total = total + jnp.sum(tile, axis=1, keepdims=True)
        mean = total * (1.0 / cols)
        for p in range(group):
            for d in range(dests):
                at = p * rows + d * share
                send_ref[d, g * group + p] = (
                    low_ref[pl.ds(at, share)] - mean[at : at + share]
                ).astype(jnp.bfloat16)
        if g > 0:
            relay(g - 1)
        send(g)
        if g + 2 < groups:
            start_halo(g + 2)

    tiles = cols // TILE

    def build(n, carry):
        base = pl.multiple_of(n * TILE, TILE)
        strip_ref[pl.ds(base, TILE)] = ramp_block(base - (tiles - 1) * TILE)
        return carry

    lax.fori_loop(0, 2 * tiles - 1, build, 0)
    relay(groups - 1)

    wide = joined * group
    size = wide * share
    for h in range(groups // joined):
        for g in range(h * joined, (h + 1) * joined):
            for a in range(ang_count):
                here = place(a, g)
                pltpu.make_async_copy(here, here, out_recv.at[a, g]).wait()
        unpack(h, planes, wide, share, ang_count, lines_ref, x_ref, rows_ref)

        def ramp(n, carry):
            start = pl.multiple_of((tiles - 1 - n) * TILE, TILE)
            value = dot(rows_ref[...], strip_ref[pl.ds(start, cols)])
            at = pl.ds(pl.multiple_of(n * TILE, TILE), TILE)
            for a in range(ang_count):
                for p in range(wide):
                    own = a * size + p * share
                    out_ref[a * planes + h * wide + p, :, at] = value[own : own + share].astype(
                        jnp.bfloat16
                    )
            return carry

        lax.fori_loop(0, tiles, ramp, 0)

    match(share, partner_ref, shifts_ref, corr_ref, x_ref, b_ref, prof_ref)

    for g in range(groups):
        for d in range(dests):

            @pl.when(jnp.logical_not(is_self(d)))
            def _():
                out_copy(d, g).wait_send()

        each_relay(lambda b, u: second_hop(b, u, g).wait_send())
        for side in range(2):

            @pl.when(has[side])
            def _():
                halo_copy(side, g).wait_send()

    for side in range(2):

        @pl.when(has[side])
        def _():
            for which in range(2):
                level_copy(side, which).wait_send()


def shards(raw_frames, dark_field, flat_field, kernel_taps, partner, shifts):
    planes, rows, cols = raw_frames.shape
    ang_count, row_devices = lax.axis_size("ang"), lax.axis_size("row")
    share = rows // ang_count
    margin = kernel_taps.shape[0] // 2
    halo = -(-margin // 16) * 16
    group = max(g for g in range(1, planes + 1) if planes % g == 0 and g * (rows + 2 * halo) <= 128)
    joined = 2 if planes // group % 2 == 0 else 1
    groups = planes // group
    out_rows, in_rows = group * rows, group * (rows + 2 * halo)
    count, half = ang_count * planes, ang_count * planes // 2
    vmem = pl.BlockSpec(memory_space=pltpu.VMEM)
    smem = pl.BlockSpec(memory_space=pltpu.SMEM)
    bf16, f32 = jnp.bfloat16, jnp.float32
    return pl.pallas_call(
        functools.partial(filter_kernel, (ang_count, row_devices, halo, group, joined)),
        out_shape=(
            jax.ShapeDtypeStruct((count, share, cols), bf16),
            jax.ShapeDtypeStruct((share, shifts.shape[0]), f32),
        ),
        in_specs=[smem, vmem, vmem, vmem, smem, vmem],
        out_specs=(vmem, vmem),
        scratch_shapes=[
            pltpu.VMEM((count, share, cols), bf16),
            pltpu.VMEM((2, planes, halo, cols), bf16),
            pltpu.VMEM((2, 2, halo, cols), bf16),
            pltpu.VMEM((rows + 2 * halo, cols), f32),
            pltpu.VMEM((rows + 2 * halo, cols), f32),
            pltpu.VMEM((2 * out_rows, in_rows), bf16),
            pltpu.VMEM((TILE + 2 * LANES, 2 * TILE), bf16),
            pltpu.VMEM((in_rows, cols), bf16),
            pltpu.VMEM((in_rows, cols), bf16),
            pltpu.VMEM((out_rows, cols + 2 * LANES), bf16),
            pltpu.VMEM((out_rows, cols + 2 * LANES), bf16),
            pltpu.VMEM((out_rows, cols), f32),
            pltpu.VMEM((ang_count, planes, share, cols), bf16),
            pltpu.VMEM((row_devices, ang_count // row_devices, planes, share, cols), bf16),
            pltpu.VMEM((2 * cols - TILE, TILE), bf16),
            pltpu.VMEM((cols // LANES, count * share, LANES), f32),
            pltpu.VMEM((ang_count * joined * group * share, cols), bf16),
            pltpu.VMEM(((cols + 2 * SPAN) // LANES, half * share, LANES), f32),
            pltpu.VMEM((share, 2 * SPAN), f32),
            pltpu.SemaphoreType.DMA((2, 2)),
            pltpu.SemaphoreType.DMA((2, 2)),
            pltpu.SemaphoreType.DMA((2, groups)),
            pltpu.SemaphoreType.DMA((2, groups)),
            pltpu.SemaphoreType.DMA((ang_count, groups)),
            pltpu.SemaphoreType.DMA((ang_count, groups)),
            pltpu.SemaphoreType.DMA((row_devices, ang_count // row_devices, groups)),
            pltpu.SemaphoreType.DMA((row_devices, ang_count // row_devices, groups)),
        ],
        compiler_params=pltpu.CompilerParams(collective_id=0, has_side_effects=True),
    )(kernel_taps, raw_frames, dark_field, flat_field, partner, shifts[None])


def solution(mesh):
    in_specs = (
        P(("scan", "ang"), "row", None),
        P("row", None),
        P("row", None),
        P(),
        P("scan"),
        P(),
    )
    out_specs = (P("scan", ("ang", "row"), None), P(("scan", "ang", "row"), None))
    return jax.shard_map(shards, mesh=mesh, in_specs=in_specs, out_specs=out_specs, check_vma=False)
```

profile of v0, /device:TPU:25, one launch (start us, length us, event | category | flops | bytes accessed | tf_op | source)
XLA Modules:
  0.0 73.2 jit_solution(7731558689719080478)
XLA Ops:
  0.6 69.0 %shard_map.77 = (bf16[48,8,2560]{2,1,0:T(8,128)(2,1)}, f32[8,256]{1,0:T(8,128)}) custom-call(f32[31]{0:T(128)} %taps_ref.1, bf16[12,32,2560]{2,1,0:T(8,128)(2,1)} %raw_ref.1, bf16[32,2560]{1,0:T(8,128)(2,1)} %dark_ref.1, bf16[32,2560]{1,0:T(8,128)(2,1)} %flat_ref.1, s32[24]{0:T(128)} %partner_ref.1, s32[1,256]{1,0:T(1,128)} %bitcast.1), custom_call_target="tpu_custom_call" | custom-call | tf_op jit(solution)/shard_map/pallas_call | solution.py:485
  69.6 0.0 copy-start
  69.6 2.9 %copy.10 = bf16[48,8,2560]{2,1,0:T(8,128)(2,1)} copy(bf16[48,8,2560]{2,1,0:T(8,128)(2,1)} %get-tuple-element.4) | data formatting | bytes 3932160
  72.6 0.0 copy-done
  72.6 0.6 copy.11
Async XLA Ops:
  69.6 3.0 %copy-start = (f32[8,256]{1,0:T(8,128)S(1)}, f32[8,256]{1,0:T(8,128)}, u32[]{:S(2)}) copy-start(f32[8,256]{1,0:T(8,128)} %get-tuple-element.5) | copy-start | bytes 24580
where the time goes:
time: 73.3 us; the launch traced here: 73.2 us
  Pallas kernels  69 us (94%)
  local copies, waits for them, and re-layouts  3.55 us (5%)
    pallas_call x1, Pallas kernels, shards(): pl.pallas_call(functools.partial(filter_kernel, (ang_count, row_devices,...  69 us
    unnamed x4, local copies, waits for them, and re-layouts  3.55 us

commit v1 on v0

v1 whole, which is shorter than its diff:
```python
import functools
import math

import jax
import jax.numpy as jnp
from jax import lax
from jax.experimental import pallas as pl
from jax.experimental.pallas import tpu as pltpu
from jax.sharding import PartitionSpec as P

SPAN = 256
LANES = 128
TILE = 256
CORES = 2
LAG = 3
MESH = pl.DeviceIdType.MESH


def split(value):
    high = value.astype(jnp.bfloat16)
    low = (value - high.astype(jnp.float32)).astype(jnp.bfloat16)
    return high, low


def band(taps_ref, lag):
    tap_count = taps_ref.shape[0]
    total = jnp.zeros(lag.shape, jnp.float32)
    for tap_index in range(tap_count):
        total = jnp.where(lag == tap_index, taps_ref[tap_index], total)
    return total


def dot(left, right):
    return jnp.dot(left, right, preferred_element_type=jnp.float32)


def ramp_block(offset):
    shape = (TILE, TILE)
    distance = (
        lax.broadcasted_iota(jnp.int32, shape, 0)
        - lax.broadcasted_iota(jnp.int32, shape, 1)
        + offset
    )
    spacing = distance.astype(jnp.float32)
    odd_distance = (distance & 1) != 0
    falloff = -4.0 / (math.pi * math.pi * jnp.maximum(spacing * spacing, 1.0))
    kernel = jnp.where(distance == 0, 1.0, jnp.where(odd_distance, falloff, 0.0))
    return kernel.astype(jnp.bfloat16)


def unpack(first, wide, planes, share, ang_count, lines_ref, x_ref, rows_ref):
    parts = x_ref.shape[0]
    size = wide * share
    for a in range(ang_count):
        start = a * planes + first
        for p in range(wide):
            line = lines_ref[start + p].astype(jnp.float32)
            for q in range(parts):
                x_ref[q, pl.ds((start + p) * share, share)] = line[:, q * LANES : (q + 1) * LANES]
        for q in range(parts):
            rows_ref[pl.ds(a * size, size), pl.ds(q * LANES, LANES)] = x_ref[
                q, pl.ds(start * share, size)
            ].astype(jnp.bfloat16)


def pair(first, end, planes, share, partner_ref, x_ref, left_ref, right_ref):
    parts, count, _ = x_ref.shape
    half = count // share // 2
    pad = SPAN // LANES
    width = end - first
    base = first * (half // planes)

    def pick(k, carry):
        a, p = k // width, k % width
        i = a * planes + (first + p + 1) % planes
        offset = partner_ref[i] - i - half
        middle = half + i

        def line(index):
            return x_ref[:, pl.ds(pl.multiple_of(index * share, share), share)]

        following = line(jnp.minimum(middle + 1, 2 * half - 1))
        chosen = jnp.where(offset > 0, following, line(middle))
        place = pl.ds(pl.multiple_of((base + k) * share, share), share)
        right_ref[pl.ds(pad, parts), place] = jnp.where(offset < 0, line(middle - 1), chosen)
        left_ref[:, place] = line(i)
        return carry

    lax.fori_loop(0, (half // planes) * width, pick, 0)


def products(r, first, end, planes, share, left_ref, right_ref):
    parts, count, _ = left_ref.shape
    pairs = count // share // planes
    pad = SPAN // LANES
    rows = pl.ds(first * pairs * share + r, (end - first) * pairs, stride=share)
    left = jnp.concatenate([left_ref[q, rows] for q in range(parts)], axis=0).astype(jnp.bfloat16)
    pieces = [right_ref[v, rows] for v in range(parts + 2 * pad)]
    last = parts - 1
    right = jnp.concatenate(
        [
            jnp.concatenate([pieces[last - q + v] for q in range(parts)], axis=0)
            for v in range(2 * pad + 1)
        ],
        axis=1,
    ).astype(jnp.bfloat16)
    return lax.dot_general(
        left, right, (((0,), (0,)), ((), ())), preferred_element_type=jnp.float32
    )


def correlate(cols, half, shifts_ref, corr_ref, prof_ref):
    lane = lax.broadcasted_iota(jnp.int32, (2 * SPAN, shifts_ref.shape[1]), 0)
    selector = (SPAN - 1 - lane == shifts_ref[...]).astype(jnp.float32)
    corr_ref[...] = jnp.dot(
        prof_ref[...],
        selector,
        precision=lax.Precision.HIGHEST,
        preferred_element_type=jnp.float32,
    ) * ((half * cols) ** -0.5)


def filter_kernel(
    sizes,
    taps_hbm,
    raw_hbm,
    dark_hbm,
    flat_hbm,
    partner_hbm,
    shifts_hbm,
    out_ref,
    corr_ref,
    taps_ref,
    partner_ref,
    shifts_ref,
    raw_ref,
    dark_ref,
    flat_ref,
    lines_ref,
    halo_ref,
    level_ref,
    dark_ext,
    gain_ext,
    row_band,
    col_band,
    x_cat,
    z_high,
    z_low,
    low_ref,
    send_ref,
    relay_ref,
    strip_ref,
    x_ref,
    rows_ref,
    left_ref,
    right_ref,
    prod_ref,
    prof_ref,
    tall_ref,
    acc_ref,
    out_stage,
    raw_sem,
    field_sem,
    write_sem,
    level_send,
    level_recv,
    halo_send,
    halo_recv,
    out_send,
    out_recv,
    relay_send,
    relay_recv,
):
    ang_count, row_devices, halo, plan = sizes
    planes, rows, cols = raw_ref.shape
    margin = taps_ref.shape[0] // 2
    dests, _, share, _ = send_ref.shape
    ext = rows + 2 * halo
    tiles = cols // TILE
    blocks = 2 * tiles - 1
    scan, ang, row = lax.axis_index("scan"), lax.axis_index("ang"), lax.axis_index("row")
    has = (row > 0, row < row_devices - 1)
    peer = (jnp.maximum(row - 1, 0), jnp.minimum(row + 1, row_devices - 1))

    def raw_copy(g):
        return pltpu.make_async_copy(raw_hbm.at[g], raw_ref.at[g], raw_sem.at[g])

    fields = (
        (taps_hbm, taps_ref),
        (dark_hbm, dark_ref),
        (flat_hbm, flat_ref),
        (partner_hbm, partner_ref),
        (shifts_hbm, shifts_ref),
    )

    def field_copy(which):
        source, target = fields[which]
        return pltpu.make_async_copy(source, target, field_sem.at[which])

    for which in range(len(fields)):
        field_copy(which).start()

    def fetch(g, carry):
        raw_copy(g).start()
        return carry

    lax.fori_loop(0, planes, fetch, 0)

    barrier = pltpu.get_barrier_semaphore()
    for a in range(ang_count):
        for b in range(row_devices):

            @pl.when(jnp.logical_or(ang != a, row != b))
            def _():
                pl.semaphore_signal(barrier, inc=1, device_id=(scan, a, b), device_id_type=MESH)

    field_copy(0).wait()
    r_out = lax.broadcasted_iota(jnp.int32, (rows, ext), 0)
    r_in = lax.broadcasted_iota(jnp.int32, (rows, ext), 1)
    high, low = split(band(taps_ref, r_in - r_out - (halo - margin)))
    row_band[:rows, :ext] = high
    row_band[:rows, ext:] = high
    row_band[rows:, :ext] = low
    row_band[rows:, ext:] = jnp.zeros((rows, ext), jnp.bfloat16)
    c_in = lax.broadcasted_iota(jnp.int32, (TILE + 2 * LANES, TILE), 0)
    c_out = lax.broadcasted_iota(jnp.int32, (TILE + 2 * LANES, TILE), 1)
    high, low = split(band(taps_ref, c_in - c_out - (LANES - margin)))
    col_band[:, :TILE] = high
    col_band[:, TILE:] = low
    for z_ref in (z_high, z_low):
        z_ref[:, :LANES] = jnp.zeros((rows, LANES), jnp.bfloat16)
        z_ref[:, LANES + cols :] = jnp.zeros((rows, LANES), jnp.bfloat16)

    for which in range(1, len(fields)):
        field_copy(which).wait()

    def wait_raw(g, carry):
        raw_copy(g).wait()
        return carry

    lax.fori_loop(0, planes, wait_raw, 0)
    pl.semaphore_wait(barrier, ang_count * row_devices - 1)

    def level_copy(side, which):
        source = (dark_ref, flat_ref)[which]
        start = 0 if side == 0 else rows - halo
        return pltpu.make_async_remote_copy(
            src_ref=source.at[pl.ds(start, halo)],
            dst_ref=level_ref.at[1 - side, which],
            send_sem=level_send.at[side, which],
            recv_sem=level_recv.at[1 - side, which],
            device_id=(scan, ang, peer[side]),
            device_id_type=MESH,
        )

    def halo_copy(side, g):
        start = 0 if side == 0 else rows - halo
        return pltpu.make_async_remote_copy(
            src_ref=raw_ref.at[g, pl.ds(start, halo)],
            dst_ref=halo_ref.at[1 - side, g],
            send_sem=halo_send.at[side],
            recv_sem=halo_recv.at[1 - side, g],
            device_id=(scan, ang, peer[side]),
            device_id_type=MESH,
        )

    def start_halo(g):
        for side in range(2):

            @pl.when(has[side])
            def _():
                halo_copy(side, g).start()

    for side in range(2):

        @pl.when(has[side])
        def _():
            for which in range(2):
                level_copy(side, which).start()

    for g in range(2):
        start_halo(g)

    def levels(dark, flat):
        dark = dark.astype(jnp.float32)
        return dark, jnp.log(flat.astype(jnp.float32) - dark)

    dark_ext[pl.ds(halo, rows)], gain_ext[pl.ds(halo, rows)] = levels(dark_ref[...], flat_ref[...])
    for side in range(2):

        @pl.when(has[side])
        def _():
            for which in range(2):
                level_copy(1 - side, which).wait_recv()

        at = 0 if side == 0 else halo + rows
        dark_ext[pl.ds(at, halo)], gain_ext[pl.ds(at, halo)] = levels(
            level_ref[side, 0], level_ref[side, 1]
        )

    upper = dests // row_devices

    def target(d):
        return upper * row + d // row_devices, d % row_devices

    def is_self(d):
        a, b = target(d)
        return jnp.logical_and(a == ang, b == row)

    def is_relayed(d):
        a, b = target(d)
        return jnp.logical_and(a != ang, b // CORES != row // CORES)

    def place(a, g):
        return lines_ref.at[a * planes + g]

    def out_copy(d, g):
        a, b = target(d)
        return pltpu.make_async_remote_copy(
            src_ref=send_ref.at[d, g],
            dst_ref=place(ang, g),
            send_sem=out_send.at[d],
            recv_sem=out_recv.at[ang, g],
            device_id=(scan, a, b),
            device_id_type=MESH,
        )

    def first_hop(d, g):
        return pltpu.make_async_remote_copy(
            src_ref=send_ref.at[d, g],
            dst_ref=relay_ref.at[row, d // row_devices, g],
            send_sem=out_send.at[d],
            recv_sem=relay_recv.at[row, d // row_devices, g],
            device_id=(scan, ang, d % row_devices),
            device_id_type=MESH,
        )

    def second_hop(b, u, g):
        return pltpu.make_async_remote_copy(
            src_ref=relay_ref.at[b, u, g],
            dst_ref=place(ang, g),
            send_sem=relay_send.at[b, u],
            recv_sem=out_recv.at[ang, g],
            device_id=(scan, upper * b + u, row),
            device_id_type=MESH,
        )

    def own_copy(d, g):
        return pltpu.make_async_copy(send_ref.at[d, g], place(ang, g), out_recv.at[ang, g])

    def relays(b, u):
        return jnp.logical_and(b // CORES != row // CORES, upper * b + u != ang)

    inner = range(1, row_devices - 1)
    outer = (0, row_devices - 1)

    def relay(sources, g):
        for b in sources:
            for u in range(upper):

                @pl.when(relays(b, u))
                def _():
                    arrived = relay_ref.at[b, u, g]
                    pltpu.make_async_copy(arrived, arrived, relay_recv.at[b, u, g]).wait()
                    second_hop(b, u, g).start()

    def send(g):
        for d in range(dests):

            @pl.when(is_relayed(d))
            def _():
                first_hop(d, g).start()

        for d in range(dests):

            @pl.when(is_self(d))
            def _():
                own_copy(d, g).start()

            @pl.when(jnp.logical_not(jnp.logical_or(is_relayed(d), is_self(d))))
            def _():
                out_copy(d, g).start()

    step = cols // 2 if cols // 2 % TILE == 0 else TILE

    def lowpass(g):
        def put(at, counts, valid):
            size = counts.shape[0]
            value = gain_ext[pl.ds(at, size)] - jnp.log(
                counts.astype(jnp.float32) - dark_ext[pl.ds(at, size)]
            )
            if valid is not None:
                value = jnp.where(valid, value, 0.0)
            high, low = split(value)
            x_cat[pl.ds(at, size)] = high
            x_cat[pl.ds(ext + at, size)] = low

        put(0, halo_ref[0, g], has[0])
        put(halo, raw_ref[g], None)
        put(halo + rows, halo_ref[1, g], has[1])

        def row_pass(n, carry):
            at = pl.multiple_of(n * step, TILE)
            both = dot(row_band[...], x_cat[:, pl.ds(at, step)])
            high, low = split(both[:rows] + both[rows:])
            to = pl.multiple_of(n * step + LANES, LANES)
            z_high[:, pl.ds(to, step)] = high
            z_low[:, pl.ds(to, step)] = low
            return carry

        lax.fori_loop(0, cols // step, row_pass, 0)

        def windows(z_ref):
            return jnp.concatenate(
                [z_ref[:, n * TILE : (n + 1) * TILE + 2 * LANES] for n in range(tiles)], axis=0
            )

        both = dot(windows(z_high), col_band[...])
        rest = dot(windows(z_low), col_band[:, :TILE])
        value = both[:, :TILE] + (both[:, TILE:] + rest)
        total = jnp.zeros((rows, 1), jnp.float32)
        for n in range(tiles):
            tile = value[n * rows : (n + 1) * rows]
            low_ref[:, n * TILE : (n + 1) * TILE] = tile
            total = total + jnp.sum(tile, axis=1, keepdims=True)
        mean = total * (1.0 / cols)
        for d in range(dests):
            at = d * share
            send_ref[d, g] = (low_ref[pl.ds(at, share)] - mean[at : at + share]).astype(
                jnp.bfloat16
            )

    def build(n, carry):
        base = pl.multiple_of(n * TILE, TILE)
        strip_ref[pl.ds(base, TILE)] = ramp_block(base - (tiles - 1) * TILE)
        return carry

    def advance(g, carry):
        for side in range(2):

            @pl.when(has[side])
            def _():
                halo_copy(1 - side, g).wait_recv()

        lowpass(g)
        send(g)

        @pl.when(g + 2 < planes)
        def _():
            start_halo(g + 2)

        each = -(-blocks // (planes - 1))
        lax.fori_loop(jnp.minimum(g * each, blocks), jnp.minimum((g + 1) * each, blocks), build, 0)

        @pl.when(g > 0)
        def _():
            relay(outer, g - 1)

        @pl.when(g >= LAG)
        def _():
            relay(inner, g - LAG)

        return carry

    def arrive(first, wide):
        for g in range(first, first + wide):
            for a in range(ang_count):
                here = place(a, g)
                pltpu.make_async_copy(here, here, out_recv.at[a, g]).wait()

    def sinogram(first, wide):
        arrive(first, wide)
        unpack(first, wide, planes, share, ang_count, lines_ref, x_ref, rows_ref)
        size = wide * share
        count = ang_count * size

        def ramp(n, carry):
            start = pl.multiple_of((tiles - 1 - n) * TILE, TILE)
            value = dot(rows_ref[:count], strip_ref[pl.ds(start, cols)])
            at = pl.ds(pl.multiple_of(n * TILE, TILE), TILE)
            for a in range(ang_count):
                for p in range(wide):
                    own = a * size + p * share
                    out_stage[a * planes + first + p, :, at] = value[own : own + share].astype(
                        jnp.bfloat16
                    )
            return carry

        lax.fori_loop(0, tiles, ramp, 0)
        for a in range(ang_count):
            write(a, first, wide).start()

    def last_sinogram(first, wide):
        arrive(first, wide)
        unpack(first, wide, planes, share, ang_count, lines_ref, x_ref, rows_ref)
        size = wide * share
        count = ang_count * size
        for k in range(tiles):
            tall_ref[k * count : (k + 1) * count] = rows_ref[:count, k * TILE : (k + 1) * TILE]
        for shift in sorted(range(1 - tiles, tiles), key=abs):
            low, high = max(0, shift), min(tiles, tiles + shift)
            block = strip_ref[(tiles - 1 + shift) * TILE : (tiles + shift) * TILE]
            value = dot(tall_ref[low * count : high * count], block)
            here = pl.ds((low - shift) * count, (high - low) * count)
            if shift:
                acc_ref[here] += value
            else:
                acc_ref[here] = value
        for n in range(tiles):
            for a in range(ang_count):
                for p in range(wide):
                    own = n * count + a * size + p * share
                    out_stage[a * planes + first + p, :, n * TILE : (n + 1) * TILE] = acc_ref[
                        own : own + share
                    ].astype(jnp.bfloat16)
        for a in range(ang_count):
            write(a, first, wide).start()

    def write(a, first, wide):
        here = pl.ds(a * planes + first, wide)
        return pltpu.make_async_copy(out_stage.at[here], out_ref.at[here], write_sem.at[a, first])

    pairs, early = ang_count * planes // 2, planes * 2 // 3
    pad = SPAN // LANES
    done, chunks, joined = 0, [], False
    for until, first, wide in plan:
        if until > done:
            lax.fori_loop(done, until, advance, 0)
            done = until
            if until == planes:
                for g in range(planes - LAG, planes):
                    relay(inner, g)
                relay(outer, planes - 1)
                for v in range(pad):
                    right_ref[v] = jnp.zeros(right_ref.shape[1:], jnp.float32)
                    right_ref[pad + cols // LANES + v] = jnp.zeros(right_ref.shape[1:], jnp.float32)
        if first + wide == planes:
            last_sinogram(first, wide)
        else:
            sinogram(first, wide)
        chunks.append((first, wide))
        if first + wide > early + 1 and not joined:
            joined = True
            pair(0, early, planes, share, partner_ref, x_ref, left_ref, right_ref)
            for r in range(share):
                prod_ref[r] = products(r, 0, early, planes, share, left_ref, right_ref)

    pair(early, planes, planes, share, partner_ref, x_ref, left_ref, right_ref)
    for r in range(share):
        product = prod_ref[r] + products(r, early, planes, planes, share, left_ref, right_ref)
        skewed = pltpu.roll(product, 0, 1, stride=1, stride_axis=0)
        prof_ref[pl.ds(r, 1)] = jnp.sum(skewed, axis=0, keepdims=True)[:, LANES:]
    correlate(cols, pairs, shifts_ref, corr_ref, prof_ref)

    for first, wide in chunks:
        for a in range(ang_count):
            write(a, first, wide).wait()

    for d in range(dests):

        @pl.when(jnp.logical_not(is_self(d)))
        def _():
            sent = send_ref.at[d]
            pltpu.make_async_copy(sent, sent, out_send.at[d]).wait()

    for b in range(row_devices):
        for u in range(upper):

            @pl.when(relays(b, u))
            def _():
                sent = relay_ref.at[b, u]
                pltpu.make_async_copy(sent, sent, relay_send.at[b, u]).wait()

    for side in range(2):

        @pl.when(has[side])
        def _():
            sent = halo_ref.at[side]
            pltpu.make_async_copy(sent, sent, halo_send.at[side]).wait()

    for side in range(2):

        @pl.when(has[side])
        def _():
            for which in range(2):
                level_copy(side, which).wait_send()


def schedule(planes):
    wide = max(planes // 3, 1)
    return (
        (planes - wide, 0, wide),
        (planes, wide, wide),
        (planes, 2 * wide, planes - 2 * wide - 1),
        (planes, planes - 1, 1),
    )


def emit_kernel(sino_ref, corr_ref, sino_out, corr_out, sems):
    a = pltpu.make_async_copy(sino_ref, sino_out, sems.at[0])
    b = pltpu.make_async_copy(corr_ref, corr_out, sems.at[1])
    a.start()
    b.start()
    a.wait()
    b.wait()


def emit(sino, corr):
    hbm = pl.BlockSpec(memory_space=pl.ANY)
    return pl.pallas_call(
        emit_kernel,
        out_shape=(jax.ShapeDtypeStruct(sino.shape, sino.dtype), jax.ShapeDtypeStruct(corr.shape, corr.dtype)),
        in_specs=[hbm, hbm],
        out_specs=(hbm, hbm),
        scratch_shapes=[pltpu.SemaphoreType.DMA((2,))],
        compiler_params=pltpu.CompilerParams(vmem_limit_bytes=2**20),
    )(sino, corr)


def shards(raw_frames, dark_field, flat_field, kernel_taps, partner, shifts):
    planes, rows, cols = raw_frames.shape
    ang_count, row_devices = lax.axis_size("ang"), lax.axis_size("row")
    share = rows // ang_count
    margin = kernel_taps.shape[0] // 2
    halo = -(-margin // 16) * 16
    ext = rows + 2 * halo
    count, half = ang_count * planes, ang_count * planes // 2
    plan = schedule(planes)
    widest = max(wide for _, _, wide in plan)
    vmem = pl.BlockSpec(memory_space=pltpu.VMEM)
    smem = pl.BlockSpec(memory_space=pltpu.SMEM)
    hbm = pl.BlockSpec(memory_space=pl.ANY)
    bf16, f32 = jnp.bfloat16, jnp.float32
    dma = pltpu.SemaphoreType.DMA
    lines, corr = pl.pallas_call(
        functools.partial(filter_kernel, (ang_count, row_devices, halo, plan)),
        out_shape=(
            jax.ShapeDtypeStruct((count, share, cols), bf16),
            jax.ShapeDtypeStruct((share, shifts.shape[0]), f32),
        ),
        in_specs=[pl.BlockSpec(memory_space=pltpu.HBM)] * 6,
        out_specs=(hbm, vmem),
        scratch_shapes=[
            pltpu.SMEM(kernel_taps.shape, f32),
            pltpu.SMEM(partner.shape, jnp.int32),
            pltpu.VMEM((1,) + shifts.shape, jnp.int32),
            pltpu.VMEM((planes, rows, cols), bf16),
            pltpu.VMEM((rows, cols), bf16),
            pltpu.VMEM((rows, cols), bf16),
            pltpu.VMEM((count, share, cols), bf16),
            pltpu.VMEM((2, planes, halo, cols), bf16),
            pltpu.VMEM((2, 2, halo, cols), bf16),
            pltpu.VMEM((ext, cols), f32),
            pltpu.VMEM((ext, cols), f32),
            pltpu.VMEM((2 * rows, 2 * ext), bf16),
            pltpu.VMEM((TILE + 2 * LANES, 2 * TILE), bf16),
            pltpu.VMEM((2 * ext, cols), bf16),
            pltpu.VMEM((rows, cols + 2 * LANES), bf16),
            pltpu.VMEM((rows, cols + 2 * LANES), bf16),
            pltpu.VMEM((rows, cols), f32),
            pltpu.VMEM((ang_count, planes, share, cols), bf16),
            pltpu.VMEM((row_devices, ang_count // row_devices, planes, share, cols), bf16),
            pltpu.VMEM((2 * cols - TILE, TILE), bf16),
            pltpu.VMEM((cols // LANES, count * share, LANES), f32),
            pltpu.VMEM((ang_count * widest * share, cols), bf16),
            pltpu.VMEM((cols // LANES, half * share, LANES), f32),
            pltpu.VMEM(((cols + 2 * SPAN) // LANES, half * share, LANES), f32),
            pltpu.VMEM((share, LANES, 2 * SPAN + LANES), f32),
            pltpu.VMEM((share, 2 * SPAN), f32),
            pltpu.VMEM((cols // TILE * ang_count * share, TILE), bf16),
            pltpu.VMEM((cols // TILE * ang_count * share, TILE), f32),
            pltpu.VMEM((count, share, cols), bf16),
            dma((planes,)),
            dma((5,)),
            dma((ang_count, planes)),
            dma((2, 2)),
            dma((2, 2)),
            dma((2,)),
            dma((2, planes)),
            dma((ang_count,)),
            dma((ang_count, planes)),
            dma((row_devices, ang_count // row_devices)),
            dma((row_devices, ang_count // row_devices, planes)),
        ],
        compiler_params=pltpu.CompilerParams(collective_id=0, has_side_effects=True, vmem_limit_bytes=40 * 2**20),
    )(*(pltpu.with_memory_space_constraint(v, pltpu.HBM) for v in (kernel_taps, raw_frames, dark_field, flat_field, partner, shifts[None])))
    return emit(lines, corr)


def solution(mesh):
    in_specs = (
        P(("scan", "ang"), "row", None),
        P("row", None),
        P("row", None),
        P(),
        P("scan"),
        P(),
    )
    out_specs = (P("scan", ("ang", "row"), None), P(("scan", "ang", "row"), None))
    return jax.shard_map(shards, mesh=mesh, in_specs=in_specs, out_specs=out_specs, check_vma=False)
```

time: 73.3 us -> 71.2 us (0.971)
  the two profiles are of different devices: /device:TPU:25 before, /device:TPU:10 now
where the time goes in v1:
time: 71.2 us; the launch traced here: 71.1 us
  Pallas kernels  70.4 us (99%)
    pallas_call x1, Pallas kernels, shards(): pl.pallas_call(functools.partial(filter_kernel, (ang_count, row_devices,...  69.1 us

profile of v1, /device:TPU:10, one launch (start us, length us, event | category | flops | bytes accessed | tf_op | source)
XLA Modules:
  0.0 71.1 jit_solution(16148517480845628339)
XLA Ops:
  0.6 69.1 %shard_map.77 = (bf16[48,8,2560]{2,1,0:T(8,128)(2,1)S(1)}, f32[8,256]{1,0:T(8,128)S(1)}) custom-call(f32[31]{0:T(128)} %taps_hbm.1, bf16[12,32,2560]{2,1,0:T(8,128)(2,1)} %raw_hbm.1, bf16[32,2560]{1,0:T(8,128)(2,1)} %dark_hbm.1, bf16[32,2560]{1,0:T(8,128)(2,1)} %flat_hbm.1, s32[24]{0:T(128)} %partner_hbm.1, s32[1,256]{1,0:T(1,128)} %bitcast.1), custom_call_target="tpu_custom_call" | custom-call | tf_op jit(solution)/shard_map/pallas_call | solution.py:635
  69.8 1.3 %shard_map.78 = (bf16[48,8,2560]{2,1,0:T(8,128)(2,1)}, f32[8,256]{1,0:T(8,128)}) custom-call(bf16[48,8,2560]{2,1,0:T(8,128)(2,1)S(1)} %get-tuple-element.4.sino_ref, f32[8,256]{1,0:T(8,128)S(1)} %get-tuple-element.5.corr_ref), custom_call_target="tpu_custom_call" | custom-call | tf_op jit(solution)/shard_map/pallas_call | solution.py:610

commit v2 on v1

--- a/solution.py
+++ b/solution.py
@@ -12,7 +12,10 @@
 LANES = 128
 TILE = 256
 CORES = 2
-LAG = 3
+HOLD = 2
+BEHIND = 5
+AHEAD = 2
+EXTRA = 0
 MESH = pl.DeviceIdType.MESH
 
 
@@ -46,21 +49,6 @@
     falloff = -4.0 / (math.pi * math.pi * jnp.maximum(spacing * spacing, 1.0))
     kernel = jnp.where(distance == 0, 1.0, jnp.where(odd_distance, falloff, 0.0))
     return kernel.astype(jnp.bfloat16)
-
-
-def unpack(first, wide, planes, share, ang_count, lines_ref, x_ref, rows_ref):
-    parts = x_ref.shape[0]
-    size = wide * share
-    for a in range(ang_count):
-        start = a * planes + first
-        for p in range(wide):
-            line = lines_ref[start + p].astype(jnp.float32)
-            for q in range(parts):
-                x_ref[q, pl.ds((start + p) * share, share)] = line[:, q * LANES : (q + 1) * LANES]
-        for q in range(parts):
-            rows_ref[pl.ds(a * size, size), pl.ds(q * LANES, LANES)] = x_ref[
-                q, pl.ds(start * share, size)
-            ].astype(jnp.bfloat16)
 
 
 def pair(first, end, planes, share, partner_ref, x_ref, left_ref, right_ref):
@@ -151,7 +139,6 @@
     relay_ref,
     strip_ref,
     x_ref,
-    rows_ref,
     left_ref,
     right_ref,
     prod_ref,
@@ -171,7 +158,7 @@
     relay_send,
     relay_recv,
 ):
-    ang_count, row_devices, halo, plan = sizes
+    ang_count, row_devices, halo = sizes
     planes, rows, cols = raw_ref.shape
     margin = taps_ref.shape[0] // 2
     dests, _, share, _ = send_ref.shape
@@ -234,11 +221,6 @@
     for which in range(1, len(fields)):
         field_copy(which).wait()
 
-    def wait_raw(g, carry):
-        raw_copy(g).wait()
-        return carry
-
-    lax.fori_loop(0, planes, wait_raw, 0)
     pl.semaphore_wait(barrier, ang_count * row_devices - 1)
 
     def level_copy(side, which):
@@ -264,10 +246,12 @@
             device_id_type=MESH,
         )
 
-    def start_halo(g):
+    far = (row % CORES == 0, row % CORES == CORES - 1)
+
+    def start_halo(g, distant):
         for side in range(2):
 
-            @pl.when(has[side])
+            @pl.when(jnp.logical_and(has[side], far[side] == distant))
             def _():
                 halo_copy(side, g).start()
 
@@ -278,8 +262,18 @@
             for which in range(2):
                 level_copy(side, which).start()
 
-    for g in range(2):
-        start_halo(g)
+    for g in range(AHEAD):
+        raw_copy(g).wait()
+        start_halo(g, True)
+    for g in range(AHEAD):
+        start_halo(g, False)
+
+    def near(g, carry):
+        raw_copy(g).wait()
+        start_halo(g, False)
+        return carry
+
+    lax.fori_loop(AHEAD, planes, near, 0)
 
     def levels(dark, flat):
         dark = dark.astype(jnp.float32)
@@ -435,6 +429,13 @@
         strip_ref[pl.ds(base, TILE)] = ramp_block(base - (tiles - 1) * TILE)
         return carry
 
+    def relay_inner(g, carry):
+        relay(inner, g)
+        return carry
+
+    def ready(g):
+        return jnp.clip(2 * (g - HOLD), 0, jnp.maximum(g, 0))
+
     def advance(g, carry):
         for side in range(2):
 
@@ -445,9 +446,14 @@
         lowpass(g)
         send(g)
 
-        @pl.when(g + 2 < planes)
-        def _():
-            start_halo(g + 2)
+        @pl.when(jnp.logical_and(g == 0, EXTRA > 0))
+        def _():
+            for more in range(EXTRA):
+                start_halo(AHEAD + more, True)
+
+        @pl.when(g + AHEAD + EXTRA < planes)
+        def _():
+            start_halo(g + AHEAD + EXTRA, True)
 
         each = -(-blocks // (planes - 1))
         lax.fori_loop(jnp.minimum(g * each, blocks), jnp.minimum((g + 1) * each, blocks), build, 0)
@@ -456,47 +462,27 @@
         def _():
             relay(outer, g - 1)
 
-        @pl.when(g >= LAG)
-        def _():
-            relay(inner, g - LAG)
-
-        return carry
-
-    def arrive(first, wide):
-        for g in range(first, first + wide):
-            for a in range(ang_count):
-                here = place(a, g)
-                pltpu.make_async_copy(here, here, out_recv.at[a, g]).wait()
-
-    def sinogram(first, wide):
-        arrive(first, wide)
-        unpack(first, wide, planes, share, ang_count, lines_ref, x_ref, rows_ref)
-        size = wide * share
-        count = ang_count * size
-
-        def ramp(n, carry):
-            start = pl.multiple_of((tiles - 1 - n) * TILE, TILE)
-            value = dot(rows_ref[:count], strip_ref[pl.ds(start, cols)])
-            at = pl.ds(pl.multiple_of(n * TILE, TILE), TILE)
-            for a in range(ang_count):
-                for p in range(wide):
-                    own = a * size + p * share
-                    out_stage[a * planes + first + p, :, at] = value[own : own + share].astype(
-                        jnp.bfloat16
-                    )
-            return carry
-
-        lax.fori_loop(0, tiles, ramp, 0)
+        lax.fori_loop(ready(g - 1), ready(g), relay_inner, 0)
+        return carry
+
+    def arrive(p):
         for a in range(ang_count):
-            write(a, first, wide).start()
-
-    def last_sinogram(first, wide):
-        arrive(first, wide)
-        unpack(first, wide, planes, share, ang_count, lines_ref, x_ref, rows_ref)
-        size = wide * share
-        count = ang_count * size
-        for k in range(tiles):
-            tall_ref[k * count : (k + 1) * count] = rows_ref[:count, k * TILE : (k + 1) * TILE]
+            here = place(a, p)
+            pltpu.make_async_copy(here, here, out_recv.at[a, p]).wait()
+
+    def sinogram(p, carry):
+        arrive(p)
+        count = ang_count * share
+        for a in range(ang_count):
+            line = lines_ref[a * planes + p].astype(jnp.float32)
+            at = pl.ds(pl.multiple_of((a * planes + p) * share, share), share)
+            for q in range(cols // LANES):
+                x_ref[q, at] = line[:, q * LANES : (q + 1) * LANES]
+            for k in range(tiles):
+                own = k * count + a * share
+                tall_ref[own : own + share] = line[:, k * TILE : (k + 1) * TILE].astype(
+                    jnp.bfloat16
+                )
         for shift in sorted(range(1 - tiles, tiles), key=abs):
             low, high = max(0, shift), min(tiles, tiles + shift)
             block = strip_ref[(tiles - 1 + shift) * TILE : (tiles + shift) * TILE]
@@ -506,55 +492,57 @@
                 acc_ref[here] += value
             else:
                 acc_ref[here] = value
-        for n in range(tiles):
-            for a in range(ang_count):
-                for p in range(wide):
-                    own = n * count + a * size + p * share
-                    out_stage[a * planes + first + p, :, n * TILE : (n + 1) * TILE] = acc_ref[
-                        own : own + share
-                    ].astype(jnp.bfloat16)
         for a in range(ang_count):
-            write(a, first, wide).start()
-
-    def write(a, first, wide):
-        here = pl.ds(a * planes + first, wide)
-        return pltpu.make_async_copy(out_stage.at[here], out_ref.at[here], write_sem.at[a, first])
-
-    pairs, early = ang_count * planes // 2, planes * 2 // 3
+            for n in range(tiles):
+                own = n * count + a * share
+                out_stage[a * planes + p, :, n * TILE : (n + 1) * TILE] = acc_ref[
+                    own : own + share
+                ].astype(jnp.bfloat16)
+            here = a * planes + p
+            pltpu.make_async_copy(out_stage.at[here], out_ref.at[here], write_sem.at[a]).start()
+        return carry
+
+    pairs = ang_count * planes // 2
     pad = SPAN // LANES
-    done, chunks, joined = 0, [], False
-    for until, first, wide in plan:
-        if until > done:
-            lax.fori_loop(done, until, advance, 0)
-            done = until
-            if until == planes:
-                for g in range(planes - LAG, planes):
-                    relay(inner, g)
-                relay(outer, planes - 1)
-                for v in range(pad):
-                    right_ref[v] = jnp.zeros(right_ref.shape[1:], jnp.float32)
-                    right_ref[pad + cols // LANES + v] = jnp.zeros(right_ref.shape[1:], jnp.float32)
-        if first + wide == planes:
-            last_sinogram(first, wide)
-        else:
-            sinogram(first, wide)
-        chunks.append((first, wide))
-        if first + wide > early + 1 and not joined:
-            joined = True
-            pair(0, early, planes, share, partner_ref, x_ref, left_ref, right_ref)
-            for r in range(share):
-                prod_ref[r] = products(r, 0, early, planes, share, left_ref, right_ref)
-
-    pair(early, planes, planes, share, partner_ref, x_ref, left_ref, right_ref)
-    for r in range(share):
-        product = prod_ref[r] + products(r, early, planes, planes, share, left_ref, right_ref)
-        skewed = pltpu.roll(product, 0, 1, stride=1, stride_axis=0)
-        prof_ref[pl.ds(r, 1)] = jnp.sum(skewed, axis=0, keepdims=True)[:, LANES:]
+    wide = max(planes // 3, 1)
+
+    def gather(part):
+        first, end = part * wide, (part + 1) * wide if part < 2 else planes
+        pair(first, end, planes, share, partner_ref, x_ref, left_ref, right_ref)
+        for r in range(share):
+            product = products(r, first, end, planes, share, left_ref, right_ref)
+            if part:
+                product = prod_ref[r] + product
+            if part < 2:
+                prod_ref[r] = product
+            else:
+                skewed = pltpu.roll(product, 0, 1, stride=1, stride_axis=0)
+                prof_ref[pl.ds(r, 1)] = jnp.sum(skewed, axis=0, keepdims=True)[:, LANES:]
+
+    def both(g, carry):
+        advance(g, carry)
+        sinogram(g - BEHIND, carry)
+        return carry
+
+    lax.fori_loop(0, BEHIND, advance, 0)
+    lax.fori_loop(BEHIND, planes, both, 0)
+    relay(outer, planes - 1)
+    lax.fori_loop(ready(planes - 1), planes, relay_inner, 0)
+    for v in range(pad):
+        right_ref[v] = jnp.zeros(right_ref.shape[1:], jnp.float32)
+        right_ref[pad + cols // LANES + v] = jnp.zeros(right_ref.shape[1:], jnp.float32)
+    if planes - BEHIND < wide + 2:
+        lax.fori_loop(planes - BEHIND, wide + 2, sinogram, 0)
+    gather(0)
+    lax.fori_loop(max(planes - BEHIND, wide + 2), 2 * wide + 2, sinogram, 0)
+    gather(1)
+    lax.fori_loop(2 * wide + 2, planes, sinogram, 0)
+    gather(2)
     correlate(cols, pairs, shifts_ref, corr_ref, prof_ref)
 
-    for first, wide in chunks:
-        for a in range(ang_count):
-            write(a, first, wide).wait()
+    for a in range(ang_count):
+        here = pl.ds(a * planes, planes)
+        pltpu.make_async_copy(out_stage.at[here], out_ref.at[here], write_sem.at[a]).wait()
 
     for d in range(dests):
 
@@ -584,16 +572,6 @@
         def _():
             for which in range(2):
                 level_copy(side, which).wait_send()
-
-
-def schedule(planes):
-    wide = max(planes // 3, 1)
-    return (
-        (planes - wide, 0, wide),
-        (planes, wide, wide),
-        (planes, 2 * wide, planes - 2 * wide - 1),
-        (planes, planes - 1, 1),
-    )
 
 
 def emit_kernel(sino_ref, corr_ref, sino_out, corr_out, sems):
@@ -625,15 +603,12 @@
     halo = -(-margin // 16) * 16
     ext = rows + 2 * halo
     count, half = ang_count * planes, ang_count * planes // 2
-    plan = schedule(planes)
-    widest = max(wide for _, _, wide in plan)
     vmem = pl.BlockSpec(memory_space=pltpu.VMEM)
-    smem = pl.BlockSpec(memory_space=pltpu.SMEM)
     hbm = pl.BlockSpec(memory_space=pl.ANY)
     bf16, f32 = jnp.bfloat16, jnp.float32
     dma = pltpu.SemaphoreType.DMA
     lines, corr = pl.pallas_call(
-        functools.partial(filter_kernel, (ang_count, row_devices, halo, plan)),
+        functools.partial(filter_kernel, (ang_count, row_devices, halo)),
         out_shape=(
             jax.ShapeDtypeStruct((count, share, cols), bf16),
             jax.ShapeDtypeStruct((share, shifts.shape[0]), f32),
@@ -662,7 +637,6 @@
             pltpu.VMEM((row_devices, ang_count // row_devices, planes, share, cols), bf16),
             pltpu.VMEM((2 * cols - TILE, TILE), bf16),
             pltpu.VMEM((cols // LANES, count * share, LANES), f32),
-            pltpu.VMEM((ang_count * widest * share, cols), bf16),
             pltpu.VMEM((cols // LANES, half * share, LANES), f32),
             pltpu.VMEM(((cols + 2 * SPAN) // LANES, half * share, LANES), f32),
             pltpu.VMEM((share, LANES, 2 * SPAN + LANES), f32),
@@ -672,7 +646,7 @@
             pltpu.VMEM((count, share, cols), bf16),
             dma((planes,)),
             dma((5,)),
-            dma((ang_count, planes)),
+            dma((ang_count,)),
             dma((2, 2)),
             dma((2, 2)),
             dma((2,)),

time: 71.2 us -> 62.3 us (0.87)
  Pallas kernels: 70.4 us -> 61.4 us
    pallas_call x1, Pallas kernels: 69.1 us -> 60.1 us  [shards(): pl.pallas_call(functools.partial(filter_kernel, (ang_count, row_devices,...]
where the time goes in v2:
time: 62.3 us; the launch traced here: 62 us
  Pallas kernels  61.4 us (99%)
  between operations  0.64 us (1%)
    pallas_call x1, Pallas kernels, shards(): pl.pallas_call(functools.partial(filter_kernel, (ang_count, row_devices,...  60.1 us
    pallas_call x1, Pallas kernels, emit(): pl.pallas_call(emit_kernel, out_shape=(jax.ShapeDtypeStruct(sino.shape, s...  1.29 us

profile of v2, /device:TPU:10, one launch (start us, length us, event | category | flops | bytes accessed | tf_op | source)
XLA Modules:
  0.0 62.0 jit_solution(1152857743888942633)
XLA Ops:
  0.6 60.1 %shard_map.77 = (bf16[48,8,2560]{2,1,0:T(8,128)(2,1)S(1)}, f32[8,256]{1,0:T(8,128)S(1)}) custom-call(f32[31]{0:T(128)} %taps_hbm.1, bf16[12,32,2560]{2,1,0:T(8,128)(2,1)} %raw_hbm.1, bf16[32,2560]{1,0:T(8,128)(2,1)} %dark_hbm.1, bf16[32,2560]{1,0:T(8,128)(2,1)} %flat_hbm.1, s32[24]{0:T(128)} %partner_hbm.1, s32[1,256]{1,0:T(1,128)} %bitcast.1), custom_call_target="tpu_custom_call" | custom-call | tf_op jit(solution)/shard_map/pallas_call | solution.py:610
  60.7 1.3 %shard_map.78 = (bf16[48,8,2560]{2,1,0:T(8,128)(2,1)}, f32[8,256]{1,0:T(8,128)}) custom-call(bf16[48,8,2560]{2,1,0:T(8,128)(2,1)S(1)} %get-tuple-element.4.sino_ref, f32[8,256]{1,0:T(8,128)S(1)} %get-tuple-element.5.corr_ref), custom_call_target="tpu_custom_call" | custom-call | tf_op jit(solution)/shard_map/pallas_call | solution.py:588

commit v3 on v2

--- a/solution.py
+++ b/solution.py
@@ -14,6 +14,10 @@
 CORES = 2
 HOLD = 2
 BEHIND = 5
+IDLE = 2
+PIECES = 1
+INNER_DIRECT = 1
+OUTER_DIRECT = 1
 AHEAD = 2
 EXTRA = 0
 MESH = pl.DeviceIdType.MESH
@@ -201,6 +205,67 @@
             def _():
                 pl.semaphore_signal(barrier, inc=1, device_id=(scan, a, b), device_id_type=MESH)
 
+    for z_ref in (z_high, z_low):
+        z_ref[:, :LANES] = jnp.zeros((rows, LANES), jnp.bfloat16)
+        z_ref[:, LANES + cols :] = jnp.zeros((rows, LANES), jnp.bfloat16)
+
+    for which in range(1, len(fields)):
+        field_copy(which).wait()
+
+    pl.semaphore_wait(barrier, ang_count * row_devices - 1)
+
+    def level_copy(side, which):
+        source = (dark_ref, flat_ref)[which]
+        start = 0 if side == 0 else rows - halo
+        return pltpu.make_async_remote_copy(
+            src_ref=source.at[pl.ds(start, halo)],
+            dst_ref=level_ref.at[1 - side, which],
+            send_sem=level_send.at[side, which],
+            recv_sem=level_recv.at[1 - side, which],
+            device_id=(scan, ang, peer[side]),
+            device_id_type=MESH,
+        )
+
+    def halo_copy(side, g):
+        start = 0 if side == 0 else rows - halo
+        return pltpu.make_async_remote_copy(
+            src_ref=raw_ref.at[g, pl.ds(start, halo)],
+            dst_ref=halo_ref.at[1 - side, g],
+            send_sem=halo_send.at[side],
+            recv_sem=halo_recv.at[1 - side, g],
+            device_id=(scan, ang, peer[side]),
+            device_id_type=MESH,
+        )
+
+    far = (row % CORES == 0, row % CORES == CORES - 1)
+
+    def start_halo(g, distant):
+        for side in range(2):
+
+            @pl.when(jnp.logical_and(has[side], far[side] == distant))
+            def _():
+                halo_copy(side, g).start()
+
+    for side in range(2):
+
+        @pl.when(has[side])
+        def _():
+            for which in range(2):
+                level_copy(side, which).start()
+
+    for g in range(AHEAD):
+        raw_copy(g).wait()
+        start_halo(g, True)
+    for g in range(AHEAD):
+        start_halo(g, False)
+
+    def near(g, carry):
+        raw_copy(g).wait()
+        start_halo(g, False)
+        return carry
+
+    lax.fori_loop(AHEAD, planes, near, 0)
+
     field_copy(0).wait()
     r_out = lax.broadcasted_iota(jnp.int32, (rows, ext), 0)
     r_in = lax.broadcasted_iota(jnp.int32, (rows, ext), 1)
@@ -214,66 +279,14 @@
     high, low = split(band(taps_ref, c_in - c_out - (LANES - margin)))
     col_band[:, :TILE] = high
     col_band[:, TILE:] = low
-    for z_ref in (z_high, z_low):
-        z_ref[:, :LANES] = jnp.zeros((rows, LANES), jnp.bfloat16)
-        z_ref[:, LANES + cols :] = jnp.zeros((rows, LANES), jnp.bfloat16)
-
-    for which in range(1, len(fields)):
-        field_copy(which).wait()
-
-    pl.semaphore_wait(barrier, ang_count * row_devices - 1)
-
-    def level_copy(side, which):
-        source = (dark_ref, flat_ref)[which]
-        start = 0 if side == 0 else rows - halo
-        return pltpu.make_async_remote_copy(
-            src_ref=source.at[pl.ds(start, halo)],
-            dst_ref=level_ref.at[1 - side, which],
-            send_sem=level_send.at[side, which],
-            recv_sem=level_recv.at[1 - side, which],
-            device_id=(scan, ang, peer[side]),
-            device_id_type=MESH,
-        )
-
-    def halo_copy(side, g):
-        start = 0 if side == 0 else rows - halo
-        return pltpu.make_async_remote_copy(
-            src_ref=raw_ref.at[g, pl.ds(start, halo)],
-            dst_ref=halo_ref.at[1 - side, g],
-            send_sem=halo_send.at[side],
-            recv_sem=halo_recv.at[1 - side, g],
-            device_id=(scan, ang, peer[side]),
-            device_id_type=MESH,
-        )
-
-    far = (row % CORES == 0, row % CORES == CORES - 1)
-
-    def start_halo(g, distant):
-        for side in range(2):
-
-            @pl.when(jnp.logical_and(has[side], far[side] == distant))
-            def _():
-                halo_copy(side, g).start()
-
-    for side in range(2):
-
-        @pl.when(has[side])
-        def _():
-            for which in range(2):
-                level_copy(side, which).start()
-
-    for g in range(AHEAD):
-        raw_copy(g).wait()
-        start_halo(g, True)
-    for g in range(AHEAD):
-        start_halo(g, False)
-
-    def near(g, carry):
-        raw_copy(g).wait()
-        start_halo(g, False)
-        return carry
-
-    lax.fori_loop(AHEAD, planes, near, 0)
+    edge = jnp.logical_or(row == 0, row == row_devices - 1)
+
+    def build(n, carry):
+        base = pl.multiple_of(n * TILE, TILE)
+        strip_ref[pl.ds(base, TILE)] = ramp_block(base - (tiles - 1) * TILE)
+        return carry
+
+    lax.fori_loop(0, jnp.where(edge, 0, blocks), build, 0)
 
     def levels(dark, flat):
         dark = dark.astype(jnp.float32)
@@ -293,6 +306,7 @@
         )
 
     upper = dests // row_devices
+    inner_hops, outer_hops = planes - INNER_DIRECT, planes - OUTER_DIRECT
 
     def target(d):
         return upper * row + d // row_devices, d % row_devices
@@ -301,9 +315,10 @@
         a, b = target(d)
         return jnp.logical_and(a == ang, b == row)
 
-    def is_relayed(d):
+    def is_relayed(d, g):
         a, b = target(d)
-        return jnp.logical_and(a != ang, b // CORES != row // CORES)
+        crosses = jnp.logical_and(a != ang, b // CORES != row // CORES)
+        return jnp.logical_and(crosses, g < jnp.where(edge, outer_hops, inner_hops))
 
     def place(a, g):
         return lines_ref.at[a * planes + g]
@@ -361,7 +376,7 @@
     def send(g):
         for d in range(dests):
 
-            @pl.when(is_relayed(d))
+            @pl.when(is_relayed(d, g))
             def _():
                 first_hop(d, g).start()
 
@@ -371,7 +386,7 @@
             def _():
                 own_copy(d, g).start()
 
-            @pl.when(jnp.logical_not(jnp.logical_or(is_relayed(d), is_self(d))))
+            @pl.when(jnp.logical_not(jnp.logical_or(is_relayed(d, g), is_self(d))))
             def _():
                 out_copy(d, g).start()
 
@@ -424,17 +439,12 @@
                 jnp.bfloat16
             )
 
-    def build(n, carry):
-        base = pl.multiple_of(n * TILE, TILE)
-        strip_ref[pl.ds(base, TILE)] = ramp_block(base - (tiles - 1) * TILE)
-        return carry
-
     def relay_inner(g, carry):
         relay(inner, g)
         return carry
 
     def ready(g):
-        return jnp.clip(2 * (g - HOLD), 0, jnp.maximum(g, 0))
+        return jnp.clip(2 * (g - HOLD), 0, jnp.clip(g, 0, inner_hops))
 
     def advance(g, carry):
         for side in range(2):
@@ -455,10 +465,12 @@
         def _():
             start_halo(g + AHEAD + EXTRA, True)
 
-        each = -(-blocks // (planes - 1))
-        lax.fori_loop(jnp.minimum(g * each, blocks), jnp.minimum((g + 1) * each, blocks), build, 0)
-
-        @pl.when(g > 0)
+        each = -(-blocks // (BEHIND - IDLE))
+        first = jnp.clip((g - IDLE) * each, 0, blocks)
+        final = jnp.clip((g - IDLE + 1) * each, 0, blocks)
+        lax.fori_loop(jnp.where(edge, first, blocks), jnp.where(edge, final, blocks), build, 0)
+
+        @pl.when(jnp.logical_and(g > 0, g <= outer_hops))
         def _():
             relay(outer, g - 1)
 
@@ -526,8 +538,9 @@
 
     lax.fori_loop(0, BEHIND, advance, 0)
     lax.fori_loop(BEHIND, planes, both, 0)
-    relay(outer, planes - 1)
-    lax.fori_loop(ready(planes - 1), planes, relay_inner, 0)
+    if outer_hops == planes:
+        relay(outer, planes - 1)
+    lax.fori_loop(ready(planes - 1), inner_hops, relay_inner, 0)
     for v in range(pad):
         right_ref[v] = jnp.zeros(right_ref.shape[1:], jnp.float32)
         right_ref[pad + cols // LANES + v] = jnp.zeros(right_ref.shape[1:], jnp.float32)
@@ -556,7 +569,8 @@
 
             @pl.when(relays(b, u))
             def _():
-                sent = relay_ref.at[b, u]
+                hops = inner_hops if b in inner else outer_hops
+                sent = relay_ref.at[b, u, pl.ds(0, hops)]
                 pltpu.make_async_copy(sent, sent, relay_send.at[b, u]).wait()
 
     for side in range(2):
@@ -575,12 +589,15 @@
 
 
 def emit_kernel(sino_ref, corr_ref, sino_out, corr_out, sems):
-    a = pltpu.make_async_copy(sino_ref, sino_out, sems.at[0])
-    b = pltpu.make_async_copy(corr_ref, corr_out, sems.at[1])
-    a.start()
-    b.start()
-    a.wait()
-    b.wait()
+    each = sino_ref.shape[0] // PIECES
+    copies = [pltpu.make_async_copy(corr_ref, corr_out, sems.at[PIECES])]
+    for n in range(PIECES):
+        part = pl.ds(n * each, each)
+        copies.append(pltpu.make_async_copy(sino_ref.at[part], sino_out.at[part], sems.at[n]))
+    for copy in copies:
+        copy.start()
+    for copy in copies:
+        copy.wait()
 
 
 def emit(sino, corr):
@@ -590,7 +607,7 @@
         out_shape=(jax.ShapeDtypeStruct(sino.shape, sino.dtype), jax.ShapeDtypeStruct(corr.shape, corr.dtype)),
         in_specs=[hbm, hbm],
         out_specs=(hbm, hbm),
-        scratch_shapes=[pltpu.SemaphoreType.DMA((2,))],
+        scratch_shapes=[pltpu.SemaphoreType.DMA((PIECES + 1,))],
         compiler_params=pltpu.CompilerParams(vmem_limit_bytes=2**20),
     )(sino, corr)
 

time: 62.3 us -> 60.3 us (0.968)
  Pallas kernels: 61.4 us -> 58.9 us
    pallas_call x1, Pallas kernels: 60.1 us -> 57.6 us  [shards(): pl.pallas_call(functools.partial(filter_kernel, (ang_count, row_devices,...]
where the time goes in v3:
time: 60.3 us; the launch traced here: 59.5 us
  Pallas kernels  58.9 us (98%)
  between operations  0.64 us (1%)
    pallas_call x1, Pallas kernels, shards(): pl.pallas_call(functools.partial(filter_kernel, (ang_count, row_devices,...  57.6 us
    pallas_call x1, Pallas kernels, emit(): pl.pallas_call(emit_kernel, out_shape=(jax.ShapeDtypeStruct(sino.shape, s...  1.29 us

profile of v3, /device:TPU:10, one launch (start us, length us, event | category | flops | bytes accessed | tf_op | source)
XLA Modules:
  0.0 59.5 jit_solution(1221261591346054993)
XLA Ops:
  0.6 57.6 %shard_map.77 = (bf16[48,8,2560]{2,1,0:T(8,128)(2,1)S(1)}, f32[8,256]{1,0:T(8,128)S(1)}) custom-call(f32[31]{0:T(128)} %taps_hbm.1, bf16[12,32,2560]{2,1,0:T(8,128)(2,1)} %raw_hbm.1, bf16[32,2560]{1,0:T(8,128)(2,1)} %dark_hbm.1, bf16[32,2560]{1,0:T(8,128)(2,1)} %flat_hbm.1, s32[24]{0:T(128)} %partner_hbm.1, s32[1,256]{1,0:T(1,128)} %bitcast.1), custom_call_target="tpu_custom_call" | custom-call | tf_op jit(solution)/shard_map/pallas_call | solution.py:627
  58.2 1.3 %shard_map.78 = (bf16[48,8,2560]{2,1,0:T(8,128)(2,1)}, f32[8,256]{1,0:T(8,128)}) custom-call(bf16[48,8,2560]{2,1,0:T(8,128)(2,1)S(1)} %get-tuple-element.4.sino_ref, f32[8,256]{1,0:T(8,128)S(1)} %get-tuple-element.5.corr_ref), custom_call_target="tpu_custom_call" | custom-call | tf_op jit(solution)/shard_map/pallas_call | solution.py:605

commit v4 on v3

--- a/solution.py
+++ b/solution.py
@@ -13,7 +13,7 @@
 TILE = 256
 CORES = 2
 HOLD = 2
-BEHIND = 5
+BEHIND = 6
 IDLE = 2
 PIECES = 1
 INNER_DIRECT = 1
@@ -470,6 +470,9 @@
         final = jnp.clip((g - IDLE + 1) * each, 0, blocks)
         lax.fori_loop(jnp.where(edge, first, blocks), jnp.where(edge, final, blocks), build, 0)
 
+        return carry
+
+    def forward(g, carry):
         @pl.when(jnp.logical_and(g > 0, g <= outer_hops))
         def _():
             relay(outer, g - 1)
@@ -523,20 +526,25 @@
         pair(first, end, planes, share, partner_ref, x_ref, left_ref, right_ref)
         for r in range(share):
             product = products(r, first, end, planes, share, left_ref, right_ref)
+            if part == 1:
+                product = prod_ref[r] + product
             if part:
-                product = prod_ref[r] + product
-            if part < 2:
+                skewed = pltpu.roll(product, 0, 1, stride=1, stride_axis=0)
+                line = jnp.sum(skewed, axis=0, keepdims=True)[:, LANES:]
+                prof_ref[pl.ds(r, 1)] = line if part == 1 else prof_ref[pl.ds(r, 1)] + line
+            else:
                 prod_ref[r] = product
-            else:
-                skewed = pltpu.roll(product, 0, 1, stride=1, stride_axis=0)
-                prof_ref[pl.ds(r, 1)] = jnp.sum(skewed, axis=0, keepdims=True)[:, LANES:]
 
     def both(g, carry):
         advance(g, carry)
         sinogram(g - BEHIND, carry)
-        return carry
-
-    lax.fori_loop(0, BEHIND, advance, 0)
+        return forward(g, carry)
+
+    def first(g, carry):
+        advance(g, carry)
+        return forward(g, carry)
+
+    lax.fori_loop(0, BEHIND, first, 0)
     lax.fori_loop(BEHIND, planes, both, 0)
     if outer_hops == planes:
         relay(outer, planes - 1)

time: 60.3 us -> 60.5 us (level)
  no operation moved by 1% of the time
where the time goes in v4:
time: 60.5 us; the launch traced here: 59.8 us
  Pallas kernels  59.2 us (98%)
  between operations  0.64 us (1%)
    pallas_call x1, Pallas kernels, shards(): pl.pallas_call(functools.partial(filter_kernel, (ang_count, row_devices,...  57.9 us
    pallas_call x1, Pallas kernels, emit(): pl.pallas_call(emit_kernel, out_shape=(jax.ShapeDtypeStruct(sino.shape, s...  1.29 us

profile of v4, /device:TPU:10, one launch (start us, length us, event | category | flops | bytes accessed | tf_op | source)
XLA Modules:
  0.0 59.8 jit_solution(6135507161949334400)
XLA Ops:
  0.6 57.9 %shard_map.77 = (bf16[48,8,2560]{2,1,0:T(8,128)(2,1)S(1)}, f32[8,256]{1,0:T(8,128)S(1)}) custom-call(f32[31]{0:T(128)} %taps_hbm.1, bf16[12,32,2560]{2,1,0:T(8,128)(2,1)} %raw_hbm.1, bf16[32,2560]{1,0:T(8,128)(2,1)} %dark_hbm.1, bf16[32,2560]{1,0:T(8,128)(2,1)} %flat_hbm.1, s32[24]{0:T(128)} %partner_hbm.1, s32[1,256]{1,0:T(1,128)} %bitcast.1), custom_call_target="tpu_custom_call" | custom-call | tf_op jit(solution)/shard_map/pallas_call | solution.py:635
  58.5 1.3 %shard_map.78 = (bf16[48,8,2560]{2,1,0:T(8,128)(2,1)}, f32[8,256]{1,0:T(8,128)}) custom-call(bf16[48,8,2560]{2,1,0:T(8,128)(2,1)S(1)} %get-tuple-element.4.sino_ref, f32[8,256]{1,0:T(8,128)S(1)} %get-tuple-element.5.corr_ref), custom_call_target="tpu_custom_call" | custom-call | tf_op jit(solution)/shard_map/pallas_call | solution.py:613

commit v5 on v3

--- a/solution.py
+++ b/solution.py
@@ -14,7 +14,7 @@
 CORES = 2
 HOLD = 2
 BEHIND = 5
-IDLE = 2
+IDLE = 1
 PIECES = 1
 INNER_DIRECT = 1
 OUTER_DIRECT = 1

time: 60.3 us -> 60.4 us (level)
  no operation moved by 1% of the time
where the time goes in v5:
time: 60.4 us; the launch traced here: 59.6 us
  Pallas kernels  59 us (98%)
  between operations  0.64 us (1%)
    pallas_call x1, Pallas kernels, shards(): pl.pallas_call(functools.partial(filter_kernel, (ang_count, row_devices,...  57.7 us
    pallas_call x1, Pallas kernels, emit(): pl.pallas_call(emit_kernel, out_shape=(jax.ShapeDtypeStruct(sino.shape, s...  1.29 us

profile of v5, /device:TPU:10, one launch (start us, length us, event | category | flops | bytes accessed | tf_op | source)
XLA Modules:
  0.0 59.6 jit_solution(18246971381307187785)
XLA Ops:
  0.6 57.7 %shard_map.77 = (bf16[48,8,2560]{2,1,0:T(8,128)(2,1)S(1)}, f32[8,256]{1,0:T(8,128)S(1)}) custom-call(f32[31]{0:T(128)} %taps_hbm.1, bf16[12,32,2560]{2,1,0:T(8,128)(2,1)} %raw_hbm.1, bf16[32,2560]{1,0:T(8,128)(2,1)} %dark_hbm.1, bf16[32,2560]{1,0:T(8,128)(2,1)} %flat_hbm.1, s32[24]{0:T(128)} %partner_hbm.1, s32[1,256]{1,0:T(1,128)} %bitcast.1), custom_call_target="tpu_custom_call" | custom-call | tf_op jit(solution)/shard_map/pallas_call | solution.py:627
  58.3 1.3 %shard_map.78 = (bf16[48,8,2560]{2,1,0:T(8,128)(2,1)}, f32[8,256]{1,0:T(8,128)}) custom-call(bf16[48,8,2560]{2,1,0:T(8,128)(2,1)S(1)} %get-tuple-element.4.sino_ref, f32[8,256]{1,0:T(8,128)S(1)} %get-tuple-element.5.corr_ref), custom_call_target="tpu_custom_call" | custom-call | tf_op jit(solution)/shard_map/pallas_call | solution.py:605
